TPU v7x, 32 devices: a whole 2x2x4 slice. The times are simulated.
32 devices in a mesh: row: 4 (over y, core), col: 8 (over z, x).
Axes of the slice: x: 2, y: 2, z: 4, core: 2. Of those that a mesh axis runs over, the one named last changes fastest.
Arguments:
- matrix: float32 [32768, 1024], P('row', 'col'), may hold values from -700 to 700, as said below
Outputs:
- r_rows: float32 [2, 128, 1024], P(None, None, 'col')
- factored: float32 [32768, 1024], P('row', 'col')
Inputs may be any that keep to these rules, and one draw needn't show every extreme that they name: `matrix`: real-valued entries.
All inputs are finite; a program needn't handle non-finite values.
Results may differ from a plain program's by a relative error of at most 0.0003.
Values sent between devices are 32-bit elements; how exact they have to be, the bound alone decides.
A program may use at most 64 MiB of HBM per device.

v0:
```python
import math
import jax
import jax.numpy as jnp
from jax import lax
from jax.sharding import PartitionSpec as P


def broadcast(block, axis, holder):
    block = jnp.where(lax.axis_index(axis) == holder, block, jnp.zeros_like(block))
    return lax.psum(block, axis)


def gram_matrix(block):
    return lax.dot_general(block, block, (((0,), (0,)), ((), ())), precision=lax.Precision.HIGHEST)


def inverse_of(lower_factor):
    width = lower_factor.shape[0]
    return jax.scipy.linalg.solve_triangular(
        lower_factor, jnp.eye(width, dtype=jnp.float32), lower=True
    )


def local(matrix):
    rows_total = matrix.shape[0] * lax.axis_size("row")
    factor_scale = math.sqrt(rows_total)
    col_index = lax.axis_index("col")
    current = matrix
    couplings = []
    stored = []
    for panel_id in range(2):
        panel_rows = broadcast(current, "col", panel_id)
        local_gram = gram_matrix(panel_rows)
        local_mixed = lax.dot_general(
            panel_rows, current, (((0,), (0,)), ((), ())), precision=lax.Precision.HIGHEST
        )
        gram_sums, mixed_sums = lax.psum((local_gram, local_mixed), "row")
        lower_factor = jnp.linalg.cholesky(gram_sums)
        inverse_lower = inverse_of(lower_factor)
        basis_rows = lax.dot_general(
            panel_rows, inverse_lower, (((1,), (1,)), ((), ())), precision=lax.Precision.HIGHEST
        )
        cross_rows = jnp.dot(inverse_lower, mixed_sums, precision=lax.Precision.HIGHEST)
        updated = current - jnp.dot(basis_rows, cross_rows, precision=lax.Precision.HIGHEST)
        scaled_basis = factor_scale * basis_rows
        current = jnp.where(col_index == panel_id, scaled_basis, updated)
        stored.append(scaled_basis)
        couplings.append(cross_rows / factor_scale)
    factored = jnp.where(col_index == 0, stored[0], current)
    return (jnp.stack(couplings), factored)


def solution(mesh):
    return jax.shard_map(
        local,
        mesh=mesh,
        in_specs=(P("row", "col"),),
        out_specs=(P(None, None, "col"), P("row", "col")),
        check_vma=False,
    )
```

profile of v0, /device:TPU:0, one launch (start us, length us, event | category | flops | bytes accessed | tf_op | source)
XLA Modules:
  0.0 509.6 jit_solution(12433639063543856480)
XLA Ops:
  7.2 0.0 all-reduce.7.cloned.1.call-start
  7.2 4.5 broadcast_select_fusion.1
  11.7 0.0 all-reduce.7.cloned.1.call-update
  11.7 0.0 all-reduce.13.cloned.1.call-start
  11.8 159.6 %all-reduce.7.cloned.1.call-done = f32[8192,128]{1,0:T(8,128)} async-done(((f32[8192,128]{1,0:T(8,128)}), f32[8192,128]{1,0:T(8,128)}) %all-reduce.7.cloned.1.call-update) | async-done | bytes 4194320 | tf_op jit(solution)/shard_map/psum | solution.py:10
  171.4 11.0 %fusion.14 = f32[128,128]{1,0:T(8,128)} fusion(f32[8192,128]{1,0:T(8,128)} %all-reduce.7.cloned.1.call-done, f32[8192,128]{1,0:T(8,128)} %param.4), kind=kOutput, calls=%fused_computation.31 | convolution fusion | flops 1610612736 | bytes 8454144 | tf_op jit(solution)/shard_map/dot_general | solution.py:34
  182.3 0.0 copy-done
  182.3 7.7 %fusion.13 = f32[128,128]{0,1:T(8,128)} fusion(f32[8192,128]{1,0:T(8,128)S(1)} %copy-done), kind=kOutput, calls=%fused_computation.30 | convolution fusion | flops 1610612736 | bytes 4259840 | tf_op jit(solution)/shard_map/dot_general | solution.py:14
  190.0 0.0 all-reduce.13.cloned.1.call-update
  190.0 0.0 all-reduce.9.cloned.1.call-start
  190.1 30.9 %all-reduce.13.cloned.1.call-done = (f32[128,128]{0,1:T(8,128)}, f32[128,128]{1,0:T(8,128)}) async-done(((f32[128,128]{0,1:T(8,128)}, f32[128,128]{1,0:T(8,128)}), (f32[128,128]{0,1:T(8,128)}, f32[128,128]{1,0:T(8,128)})) %all-reduce.13.cloned.1.call-update) | async-done | bytes 131088 | tf_op jit(solution)/shard_map/psum | solution.py:37
  221.0 0.9 copy.4
  222.0 0.9 fusion.12
  222.8 11.7 %cholesky.44 = f32[128,128]{1,0:T(8,128)S(1)} custom-call(f32[128,128]{1,0:T(8,128)S(1)} %fusion.12), custom_call_target="Cholesky" | custom-call | tf_op jit(solution)/shard_map/jit(cholesky)/cholesky | solution.py:38
  234.6 0.6 compare_reduce_fusion.1
  235.2 0.7 fusion.7
  235.9 9.8 %custom-call.6 = f32[1,128,128]{1,2,0:T(8,128)S(1)} custom-call(f32[1,128,128]{2,1,0:T(8,128)S(1)} %fusion.7), custom_call_target="InvertDiagBlocksLowerTriangular" | custom-call | tf_op jit(solution)/shard_map/jit(_solve_triangular)/triangular_solve | solution.py:19
  245.7 0.3 fusion.5
  246.0 1.0 fusion.15
  247.0 0.0 copy-start.4
  247.0 5.5 %fusion.16 = f32[8192,128]{1,0:T(8,128)S(1)} fusion(f32[8192,128]{1,0:T(8,128)} %all-reduce.7.cloned.1.call-done, f32[128,128]{1,0:T(8,128)S(1)} %fusion.5), kind=kOutput, calls=%fused_computation.33 | convolution fusion | flops 1610612736 | bytes 8454144 | tf_op jit(solution)/shard_map/dot_general | solution.py:40
  252.5 0.0 copy-done.4
  252.6 0.0 copy-start.2
  252.6 5.8 %broadcast_select_fusion = (f32[8192,128]{1,0:T(8,128)}, f32[8192,128]{1,0:T(8,128)}) fusion(pred[]{:T(512)S(6)} %eq.17, f32[8192,128]{1,0:T(8,128)S(1)} %copy-done.4, f32[8192,128]{1,0:T(8,128)S(1)} %fusion.16, f32[128,128]{1,0:T(8,128)S(1)} %fusion.15, pred[]{:T(512)S(6)} %eq.15), kind=kOutput, calls=%fused_computation.5 | convolution fusion | flops 1614807040 | bytes 16842754 | tf_op jit(solution)/shard_map/dot_general | solution.py:44
  258.4 0.0 copy-done.2
  258.4 0.0 all-reduce.9.cloned.1.call-update
  258.4 0.2 all-reduce.11.cloned.1.call-start
  258.7 156.3 %all-reduce.9.cloned.1.call-done = f32[8192,128]{1,0:T(8,128)} async-done(((f32[8192,128]{1,0:T(8,128)}), f32[8192,128]{1,0:T(8,128)}) %all-reduce.9.cloned.1.call-update) | async-done | bytes 4194320 | tf_op jit(solution)/shard_map/psum | solution.py:10
  415.0 11.0 %fusion.17 = f32[128,128]{0,1:T(8,128)} fusion(f32[8192,128]{1,0:T(8,128)} %all-reduce.9.cloned.1.call-done), kind=kOutput, calls=%fused_computation.34 | convolution fusion | flops 1610612736 | bytes 4259840 | tf_op jit(solution)/shard_map/dot_general | solution.py:14
  426.0 0.0 copy-done.1
  426.0 0.0 copy-done.5
  426.0 7.6 %fusion.18 = f32[128,128]{1,0:T(8,128)} fusion(f32[8192,128]{1,0:T(8,128)S(1)} %copy-done.1, f32[8192,128]{1,0:T(8,128)S(1)} %copy-done.5), kind=kOutput, calls=%fused_computation.35 | convolution fusion | flops 1610612736 | bytes 8454144 | tf_op jit(solution)/shard_map/dot_general | solution.py:34
  433.5 0.0 all-reduce.11.cloned.1.call-update
  433.6 31.0 %all-reduce.11.cloned.1.call-done = (f32[128,128]{0,1:T(8,128)}, f32[128,128]{1,0:T(8,128)}) async-done(((f32[128,128]{0,1:T(8,128)}, f32[128,128]{1,0:T(8,128)}), (f32[128,128]{0,1:T(8,128)}, f32[128,128]{1,0:T(8,128)})) %all-reduce.11.cloned.1.call-update) | async-done | bytes 131088 | tf_op jit(solution)/shard_map/psum | solution.py:37
  464.6 0.9 copy.6
  465.5 0.9 fusion.10
  466.4 11.7 %cholesky.55 = f32[128,128]{1,0:T(8,128)S(1)} custom-call(f32[128,128]{1,0:T(8,128)S(1)} %fusion.10), custom_call_target="Cholesky" | custom-call | tf_op jit(solution)/shard_map/jit(cholesky)/cholesky | solution.py:38
  478.1 0.6 compare_reduce_fusion
  478.7 0.7 fusion.8
  479.4 9.8 %custom-call.7 = f32[1,128,128]{1,2,0:T(8,128)S(1)} custom-call(f32[1,128,128]{2,1,0:T(8,128)S(1)} %fusion.8), custom_call_target="InvertDiagBlocksLowerTriangular" | custom-call | tf_op jit(solution)/shard_map/jit(_solve_triangular)/triangular_solve | solution.py:19
  489.2 0.3 fusion.3
  489.5 1.0 fusion.19
  490.6 0.0 copy-start.3
  490.6 0.0 copy-start.6
  490.6 5.7 %fusion.20 = f32[8192,128]{1,0:T(8,128)S(1)} fusion(f32[8192,128]{1,0:T(8,128)} %all-reduce.9.cloned.1.call-done, f32[128,128]{1,0:T(8,128)S(1)} %fusion.3), kind=kOutput, calls=%fused_computation.37 | convolution fusion | flops 1610612736 | bytes 8454144 | tf_op jit(solution)/shard_map/dot_general | solution.py:40
  496.4 0.0 copy-done.3
  496.4 5.6 %fusion.2 = f32[8192,128]{1,0:T(8,128)} fusion(f32[8192,128]{1,0:T(8,128)S(1)} %copy-done.6, f32[8192,128]{1,0:T(8,128)S(1)} %fusion.20, f32[128,128]{1,0:T(8,128)S(1)} %fusion.19, f32[8192,128]{1,0:T(8,128)S(1)} %copy-done.3, pred[]{:T(512)S(6)} %eq.17, pred[]{:T(512)S(6)} %eq.15), kind=kOutput, calls=%fused_computation.4 | convolution fusion | flops 1615855616 | bytes 16842754 | tf_op jit(solution)/shard_map/dot_general | solution.py:44
  502.0 0.7 pad_maximum_fusion
  (8 shorter events, 0.1 us)
Async XLA Ops:
  7.2 164.2 %all-reduce.7.cloned.1.call-start = ((), (), s32[]{:S(2)}) async-start(), calls=%async_computation | async-start | bytes 8388608 | tf_op jit(solution)/shard_map/psum | solution.py:10
  11.7 209.3 %all-reduce.13.cloned.1.call-start = ((), (), s32[]{:S(2)}) async-start(), calls=%async_computation.3 | async-start | bytes 262144 | tf_op jit(solution)/shard_map/psum | solution.py:37
  171.4 11.0 %copy-start = (f32[8192,128]{1,0:T(8,128)S(1)}, f32[8192,128]{1,0:T(8,128)}, u32[]{:S(2)}) copy-start(f32[8192,128]{1,0:T(8,128)} %all-reduce.7.cloned.1.call-done) | copy-start | bytes 12582916
  190.0 225.0 %all-reduce.9.cloned.1.call-start = ((), (), s32[]{:S(2)}) async-start(), calls=%async_computation.1 | async-start | bytes 8388608 | tf_op jit(solution)/shard_map/psum | solution.py:10
  247.0 5.5 %copy-start.4 = (f32[8192,128]{1,0:T(8,128)S(1)}, f32[8192,128]{1,0:T(8,128)}, u32[]{:S(2)}) copy-start(f32[8192,128]{1,0:T(8,128)} %param.4) | copy-start | bytes 12582916
  252.6 5.9 %copy-start.2 = (f32[8192,128]{1,0:T(8,128)}, f32[8192,128]{1,0:T(8,128)S(1)}, u32[]{:S(2)}) copy-start(f32[8192,128]{1,0:T(8,128)S(1)} %fusion.16) | copy-start | bytes 12582916
  258.4 206.1 %all-reduce.11.cloned.1.call-start = ((), (), s32[]{:S(2)}) async-start(), calls=%async_computation.2 | async-start | bytes 262144 | tf_op jit(solution)/shard_map/psum | solution.py:37
  415.0 11.0 %copy-start.1 = (f32[8192,128]{1,0:T(8,128)S(1)}, f32[8192,128]{1,0:T(8,128)}, u32[]{:S(2)}) copy-start(f32[8192,128]{1,0:T(8,128)} %all-reduce.9.cloned.1.call-done) | copy-start | bytes 12582916
  415.0 11.0 %copy-start.5 = (f32[8192,128]{1,0:T(8,128)S(1)}, f32[8192,128]{1,0:T(8,128)}, u32[]{:S(2)}) copy-start(f32[8192,128]{1,0:T(8,128)} %get-tuple-element.9) | copy-start | bytes 12582916
  490.6 5.8 %copy-start.3 = (f32[8192,128]{1,0:T(8,128)S(1)}, f32[8192,128]{1,0:T(8,128)}, u32[]{:S(2)}) copy-start(f32[8192,128]{1,0:T(8,128)} %copy-done.2) | copy-start | bytes 12582916
  490.6 5.8 %copy-start.6 = (f32[8192,128]{1,0:T(8,128)S(1)}, f32[8192,128]{1,0:T(8,128)}, u32[]{:S(2)}) copy-start(f32[8192,128]{1,0:T(8,128)} %get-tuple-element.9) | copy-start | bytes 12582916
Sparse Core Ops, SparseCore 0:
  12.2 159.0 all-reduce.6
  190.2 30.8 all-reduce.12
  258.6 156.3 all-reduce.8
  433.7 30.8 all-reduce.10
where the time goes:
time: 519 us; the launch traced here: 510 us
  waiting for transfers between devices  378 us (73%)
  matrix products  62.5 us (12%)
  other arithmetic  52.6 us (10%)
  between operations  14.4 us (3%)
    psum x2, waiting for transfers between devices, broadcast(): return lax.psum(block, axis)  316 us
    psum x2, waiting for transfers between devices, local(): gram_sums, mixed_sums = lax.psum((local_gram, local_mixed), 'row')  61.9 us
    another operation x6, other arithmetic, local(): lower_factor = jnp.linalg.cholesky(gram_sums)  24.8 us
    another operation x4, other arithmetic, inverse_of(): jax.scipy.linalg.solve_triangular(lower_factor, jnp.eye(width, dtype=jnp....  20.9 us
    dot_general x2, matrix products, gram_matrix(): lax.dot_general(block, block, (((0,), (0,)), ((), ())), precision=lax.Pre...  18.7 us
    dot_general x2, matrix products, local(): lax.dot_general(panel_rows, current, (((0,), (0,)), ((), ())), precision=...  18.5 us
    dot_general x2, matrix products, local(): jnp.dot(basis_rows, cross_rows, precision=lax.Precision.HIGHEST)  11.4 us
    dot_general x2, matrix products, local(): lax.dot_general(panel_rows, inverse_lower, (((1,), (1,)), ((), ())), prec...  11.2 us
  transfers between devices with their start and end apart: 4, of which 4 were waited for; matrix products, arithmetic and copies ran while one was open for 0% of the time, Pallas kernels for 0%

commit v1 on v0

--- a/solution.py
+++ b/solution.py
@@ -7,7 +7,7 @@
 
 def broadcast(block, axis, holder):
     block = jnp.where(lax.axis_index(axis) == holder, block, jnp.zeros_like(block))
-    return lax.psum(block, axis)
+    return jnp.sum(lax.all_gather(block, axis), axis=0)
 
 
 def gram_matrix(block):

time: 519 us -> 1510 us (2.91)
  waiting for transfers between devices: 378 us -> 1340 us
  other arithmetic: 52.6 us -> 80.7 us
    all_gather x0 -> x2, waiting for transfers between devices: none -> 1280 us  [broadcast(): return jnp.sum(lax.all_gather(block, axis), axis=0)]
    psum x2 -> x0, waiting for transfers between devices: 316 us -> none  [broadcast(): return lax.psum(block, axis)]
    reduce_sum x0 -> x2, other arithmetic: none -> 28.1 us  [broadcast(): return jnp.sum(lax.all_gather(block, axis), axis=0)]
where the time goes in v1:
time: 1510 us; the launch traced here: 1500 us
  waiting for transfers between devices  1340 us (89%)
  other arithmetic  80.7 us (5%)
  matrix products  60.6 us (4%)
    all_gather x2, waiting for transfers between devices, broadcast(): return jnp.sum(lax.all_gather(block, axis), axis=0)  1280 us
    psum x2, waiting for transfers between devices, local(): gram_sums, mixed_sums = lax.psum((local_gram, local_mixed), 'row')  63.8 us
  transfers between devices with their start and end apart: 4, of which 4 were waited for; matrix products, arithmetic and copies ran while one was open for 0% of the time, Pallas kernels for 0%

profile of v1, /device:TPU:0, one launch (start us, length us, event | category | flops | bytes accessed | tf_op | source)
XLA Modules:
  0.0 1498.1 jit_solution(12705838416168049127)
XLA Ops:
  7.2 0.0 all-gather.5.cloned.1.call-start
  7.2 4.5 broadcast_select_fusion.1
  11.7 0.0 all-gather.5.cloned.1.call-update
  11.7 0.0 all-reduce.7.cloned.1.call-start
  11.8 638.7 %all-gather.5.cloned.1.call-done = f32[65536,128]{1,0:T(8,128)} async-done(((f32[8192,128]{1,0:T(8,128)}), f32[65536,128]{1,0:T(8,128)}) %all-gather.5.cloned.1.call-update) | async-done | bytes 33554448 | tf_op jit(solution)/shard_map/all_gather | solution.py:10
  650.5 14.0 reduce_sum.18
  664.5 11.0 fusion.14
  675.4 0.0 copy-done
  675.4 7.7 fusion.13
  683.1 0.0 all-reduce.7.cloned.1.call-update
  683.2 0.0 all-gather.7.cloned.1.call-start
  683.2 31.9 %all-reduce.7.cloned.1.call-done = (f32[128,128]{0,1:T(8,128)}, f32[128,128]{1,0:T(8,128)}) async-done(((f32[128,128]{0,1:T(8,128)}, f32[128,128]{1,0:T(8,128)}), (f32[128,128]{0,1:T(8,128)}, f32[128,128]{1,0:T(8,128)})) %all-reduce.7.cloned.1.call-update) | async-done | bytes 131088 | tf_op jit(solution)/shard_map/psum | solution.py:37
  715.1 0.9 copy.4
  716.0 0.9 fusion.12
  716.9 11.7 cholesky.44
  728.6 0.6 compare_reduce_fusion.1
  729.3 0.7 fusion.7
  729.9 9.8 custom-call.6
  739.8 0.3 fusion.5
  740.0 0.0 copy-start.7
  740.1 0.0 copy-start.4
  740.1 5.5 fusion.16
  745.6 0.0 copy-start.2
  745.6 0.0 copy-done.7
  745.6 0.2 fusion.15
  745.8 5.8 broadcast_select_fusion
  751.7 0.0 all-gather.7.cloned.1.call-update
  751.7 0.0 all-reduce.5.cloned.1.call-start
  751.7 637.8 %all-gather.7.cloned.1.call-done = f32[65536,128]{1,0:T(8,128)} async-done(((f32[8192,128]{1,0:T(8,128)}), f32[65536,128]{1,0:T(8,128)}) %all-gather.7.cloned.1.call-update) | async-done | bytes 33554448 | tf_op jit(solution)/shard_map/all_gather | solution.py:10
  1389.5 14.2 reduce_sum.19
  1403.7 11.0 fusion.17
  1414.6 0.0 copy-done.1
  1414.6 7.6 fusion.18
  1422.2 0.0 all-reduce.5.cloned.1.call-update
  1422.2 31.9 %all-reduce.5.cloned.1.call-done = (f32[128,128]{0,1:T(8,128)}, f32[128,128]{1,0:T(8,128)}) async-done(((f32[128,128]{0,1:T(8,128)}, f32[128,128]{1,0:T(8,128)}), (f32[128,128]{0,1:T(8,128)}, f32[128,128]{1,0:T(8,128)})) %all-reduce.5.cloned.1.call-update) | async-done | bytes 131088 | tf_op jit(solution)/shard_map/psum | solution.py:37
  1454.1 0.9 copy.6
  1455.1 0.9 fusion.10
  1455.9 11.7 cholesky.55
  1467.7 0.6 compare_reduce_fusion
  1468.3 0.7 fusion.8
  1469.0 9.8 custom-call.7
  1478.8 0.3 fusion.3
  1479.1 5.5 fusion.20
  1484.6 0.2 fusion.19
  1484.9 0.0 copy-done.3
  1484.9 0.0 copy-done.6
  1484.9 5.6 fusion.2
  1490.5 0.7 pad_maximum_fusion
  (14 shorter events, 0.1 us)
Async XLA Ops:
  7.2 643.3 %all-gather.5.cloned.1.call-start = ((), (), s32[]{:S(2)}) async-start(), calls=%async_computation | async-start | bytes 37748736 | tf_op jit(solution)/shard_map/all_gather | solution.py:10
  11.7 703.4 %all-reduce.7.cloned.1.call-start = ((), (), s32[]{:S(2)}) async-start(), calls=%async_computation.3 | async-start | bytes 262144 | tf_op jit(solution)/shard_map/psum | solution.py:37
  664.5 11.0 copy-start
  683.2 706.3 %all-gather.7.cloned.1.call-start = ((), (), s32[]{:S(2)}) async-start(), calls=%async_computation.1 | async-start | bytes 37748736 | tf_op jit(solution)/shard_map/all_gather | solution.py:10
  740.0 5.5 copy-start.7
  740.1 5.7 copy-start.4
  745.6 6.1 copy-start.2
  751.7 702.5 %all-reduce.5.cloned.1.call-start = ((), (), s32[]{:S(2)}) async-start(), calls=%async_computation.2 | async-start | bytes 262144 | tf_op jit(solution)/shard_map/psum | solution.py:37
  1403.7 11.0 copy-start.1
  1403.7 11.0 copy-start.5
  1479.1 5.5 copy-start.8
  1479.1 5.8 copy-start.3
  1479.1 5.8 copy-start.6
Sparse Core Ops, SparseCore 0:
  11.8 638.6 all-gather.4
  683.3 31.7 all-reduce.6
  751.8 637.6 all-gather.6
  1422.3 31.7 all-reduce.4
